TPU v7x, 512 devices: a whole 4x4x16 slice. The times are simulated.
512 devices in a mesh: feat: 64 (over x, z_hi, y, core), tok: 8 (over z_lo).
Axes of the slice: x: 4, y: 4, z: 16 (z_hi: 2, z_lo: 8; z = z_hi * 8 + z_lo), core: 2. Of those that a mesh axis runs over, the one named last changes fastest.
Arguments:
- features: bfloat16 [1024, 131072], P('tok', 'feat'), may hold values from -6 to 6
- signs: int32 [131072], P('feat'), may hold values from -1 to 1, as said below
- columns: int32 [1024], replicated, may hold values from 0 to 131071, as said below
- labels: int32 [1024, 1], P('tok'), may hold values from 0 to 31; in each aligned block of 128 rows (0 to 127, 128 to 255, ...) at most 8 rows name the same one
Outputs:
- gram: float32 [32, 1024, 1024], P('tok', 'feat')
Inputs may be any that keep to these rules, and one draw needn't show every extreme that they name: `signs`: every entry is -1 or 1. `columns`: the 1024 indices are distinct. `labels`: among the rows of one device no concept appears more than 8 times.
All inputs are finite; a program needn't handle non-finite values.
Results may differ from a plain program's by a relative error of at most 0.004.
Values may be sent and summed in bfloat16 or wider, within the bound.
A program may use at most 64 MiB of HBM per device.

v0:
```python
import math
import jax
import jax.numpy as jnp
from jax import lax
from jax.sharding import PartitionSpec as P

C = 32


def from_partner(array, axis, distance):
    return lax.ppermute(array, axis, [(i, i ^ 1 << distance) for i in range(lax.axis_size(axis))])


def bit_parity(number, bit_count):
    total = jnp.zeros_like(number)
    for position in range(bit_count):
        total = total ^ number >> position & 1
    return total


def sylvester(order, dtype):
    index = lax.iota(jnp.int32, order)
    parity = bit_parity(index[:, None] & index[None, :], order.bit_length())
    return (1 - 2 * parity).astype(dtype)


def body(features, signs, columns, labels):
    rows, width = features.shape
    feat_count = lax.axis_size("feat")
    feat_index = lax.axis_index("feat")
    tok_count = lax.axis_size("tok")
    kept = columns.shape[0]
    shard_cols = kept // feat_count
    flat_labels = labels[:, 0]
    signed = features * signs.astype(jnp.bfloat16)[None, :]
    transformed = jnp.dot(
        signed, sylvester(width, jnp.bfloat16), preferred_element_type=jnp.float32
    )
    local_col = columns % width
    owner = columns // width
    sections = feat_count.bit_length() - 1
    for section in range(sections):
        partner = from_partner(transformed, "feat", section)
        upper = feat_index >> section & 1 == 1
        transformed = jnp.where(upper, partner - transformed, transformed + partner)
    picked = jnp.take(transformed, local_col, axis=1)
    owned = (owner == feat_index)[None, :]
    combined = lax.psum(jnp.where(owned, picked, 0.0), "feat")
    sketch = (combined * (1.0 / math.sqrt(width * feat_count))).astype(jnp.bfloat16)
    factor = C / (rows * tok_count)
    own_rows = lax.dynamic_slice_in_dim(sketch, feat_index * shard_cols, shard_cols, 1)
    wanted = lax.iota(jnp.int32, C // tok_count * lax.axis_size("tok"))
    onehot = (flat_labels[:, None] == wanted[None, :]).astype(jnp.bfloat16)
    weighted = (onehot[:, :, None] * own_rows[:, None, :]).reshape(
        rows, C // tok_count * lax.axis_size("tok") * shard_cols
    )
    partial_gram = jnp.einsum("rm,rk->mk", weighted, sketch, preferred_element_type=jnp.float32)
    return lax.psum_scatter(
        partial_gram.reshape(C // tok_count * lax.axis_size("tok"), shard_cols, kept) * factor,
        "tok",
        scatter_dimension=0,
        tiled=True,
    )


def solution(mesh):
    in_specs = (P("tok", "feat"), P("feat"), P(), P("tok", None))
    out_specs = P("tok", "feat", None)
    return jax.shard_map(body, mesh=mesh, in_specs=in_specs, out_specs=out_specs, check_vma=False)
```

profile of v0, /device:TPU:12, one launch (start us, length us, event | category | flops | bytes accessed | tf_op | source)
XLA Modules:
  0.0 1409.9 jit_solution(11742431662747528848)
XLA Ops:
  6.5 0.7 convert_element_type.17
  7.2 23.5 %fusion = f32[128,2048]{1,0:T(8,128)S(1)} fusion(bf16[128,2048]{1,0:T(8,128)(2,1)} %param.4, bf16[2048]{0:T(1024)(128)(2,1)S(1)} %convert_element_type.17), kind=kOutput, calls=%fused_computation.2 | convolution fusion | flops 1237581824 | bytes 1576960 | tf_op jit(solution)/shard_map/dot_general | solution.py:36
  30.8 1.9 collective-permute-start
  32.7 2.6 collective-permute-done
  35.5 2.4 collective-permute-start.1
  37.8 24.7 %collective-permute-done.1 = f32[128,2048]{1,0:T(8,128)S(1)} collective-permute-done((f32[128,2048]{1,0:T(8,128)S(1)}, f32[128,2048]{1,0:T(8,128)S(1)}, u32[]{:S(2)}, u32[]{:S(2)}) %collective-permute-start.1) | collective-permute-done | bytes 1048608 | tf_op jit(solution)/shard_map/ppermute | solution.py:11
  62.6 0.1 add_select_fusion.4
  62.7 4.2 collective-permute-start.2
  66.9 23.6 %collective-permute-done.2 = f32[128,2048]{1,0:T(8,128)S(1)} collective-permute-done((f32[128,2048]{1,0:T(8,128)S(1)}, f32[128,2048]{1,0:T(8,128)S(1)}, u32[]{:S(2)}, u32[]{:S(2)}) %collective-permute-start.2) | collective-permute-done | bytes 1048608 | tf_op jit(solution)/shard_map/ppermute | solution.py:11
  90.6 15.7 %collective-permute-start.3 = (f32[128,2048]{1,0:T(8,128)S(1)}, f32[128,2048]{1,0:T(8,128)S(1)}, u32[]{:S(2)}, u32[]{:S(2)}) collective-permute-start(f32[128,2048]{1,0:T(8,128)S(1)} %add_select_fusion.3), channel_id=1, source_target_pairs={{0,64},{8,72},{16,80},{24,88},{32,96},{40,104},{48,112},{56,120},{... | collective-permute-start | bytes 3145736 | tf_op jit(solution)/shard_map/ppermute | solution.py:11
  106.4 35.5 %collective-permute-done.3 = f32[128,2048]{1,0:T(8,128)S(1)} collective-permute-done((f32[128,2048]{1,0:T(8,128)S(1)}, f32[128,2048]{1,0:T(8,128)S(1)}, u32[]{:S(2)}, u32[]{:S(2)}) %collective-permute-start.3) | collective-permute-done | bytes 1048608 | tf_op jit(solution)/shard_map/ppermute | solution.py:11
  141.9 0.1 add_select_fusion.2
  142.1 3.1 collective-permute-start.4
  145.2 21.3 %collective-permute-done.4 = f32[128,2048]{1,0:T(8,128)S(1)} collective-permute-done((f32[128,2048]{1,0:T(8,128)S(1)}, f32[128,2048]{1,0:T(8,128)S(1)}, u32[]{:S(2)}, u32[]{:S(2)}) %collective-permute-start.4) | collective-permute-done | bytes 1048608 | tf_op jit(solution)/shard_map/ppermute | solution.py:11
  166.6 14.8 %collective-permute-start.5 = (f32[128,2048]{1,0:T(8,128)S(1)}, f32[128,2048]{1,0:T(8,128)S(1)}, u32[]{:S(2)}, u32[]{:S(2)}) collective-permute-start(f32[128,2048]{1,0:T(8,128)S(1)} %add_select_fusion.1), channel_id=1, source_target_pairs={{0,256},{8,264},{16,272},{24,280},{32,288},{40,296},{48,304},{56,3... | collective-permute-start | bytes 3145736 | tf_op jit(solution)/shard_map/ppermute | solution.py:11
  181.5 20.4 %collective-permute-done.5 = f32[128,2048]{1,0:T(8,128)S(1)} collective-permute-done((f32[128,2048]{1,0:T(8,128)S(1)}, f32[128,2048]{1,0:T(8,128)S(1)}, u32[]{:S(2)}, u32[]{:S(2)}) %collective-permute-start.5) | collective-permute-done | bytes 1048608 | tf_op jit(solution)/shard_map/ppermute | solution.py:11
  202.1 0.3 copy.5
  202.4 2.8 gather_fusion
  205.3 0.2 copy.6
  205.5 0.8 select_bitcast_fusion
  206.4 1084.6 %all-reduce.2.cloned.1.call-done = f32[128,1024]{1,0:T(8,128)} async-done(((f32[128,1024]{1,0:T(8,128)}), f32[128,1024]{1,0:T(8,128)}) %all-reduce.2.cloned.1.call-update) | async-done | bytes 524304 | tf_op jit(solution)/shard_map/psum | solution.py:48
  1291.0 1.1 multiply_convert_fusion
  1292.2 1.8 convolution_multiply_fusion
  1294.0 109.1 %reduce-scatter.2.cloned.1.call-done = f32[4,16,1024]{2,1,0:T(8,128)} async-done(((f32[32,16,1024]{2,1,0:T(8,128)}), f32[4,16,1024]{2,1,0:T(8,128)}) %reduce-scatter.2.cloned.1.call-update) | async-done | bytes 262160 | tf_op jit(solution)/shard_map/reduce_scatter | solution.py:58
  (17 shorter events, 0.9 us)
Async XLA Ops:
  6.5 1284.4 %all-reduce.2.cloned.1.call-start = ((), (), s32[]{:S(2)}) async-start(), calls=%async_computation.1 | async-start | bytes 1048576 | tf_op jit(solution)/shard_map/psum | solution.py:48
  30.8 4.6 collective-permute-start
  35.5 27.1 %collective-permute-start.1 = (f32[128,2048]{1,0:T(8,128)S(1)}, f32[128,2048]{1,0:T(8,128)S(1)}, u32[]{:S(2)}, u32[]{:S(2)}) collective-permute-start(f32[128,2048]{1,0:T(8,128)S(1)} %add_select_fusion.5), channel_id=1, source_target_pairs={{0,16},{8,24},{16,0},{24,8},{32,48},{40,56},{48,32},{56,40},{64,80... | collective-permute-start | bytes 3145736 | tf_op jit(solution)/shard_map/ppermute | solution.py:11
  62.7 27.8 %collective-permute-start.2 = (f32[128,2048]{1,0:T(8,128)S(1)}, f32[128,2048]{1,0:T(8,128)S(1)}, u32[]{:S(2)}, u32[]{:S(2)}) collective-permute-start(f32[128,2048]{1,0:T(8,128)S(1)} %add_select_fusion.4), channel_id=1, source_target_pairs={{0,32},{8,40},{16,48},{24,56},{32,0},{40,8},{48,16},{56,24},{64,96... | collective-permute-start | bytes 3145736 | tf_op jit(solution)/shard_map/ppermute | solution.py:11
  90.6 51.2 %collective-permute-start.3 = (f32[128,2048]{1,0:T(8,128)S(1)}, f32[128,2048]{1,0:T(8,128)S(1)}, u32[]{:S(2)}, u32[]{:S(2)}) collective-permute-start(f32[128,2048]{1,0:T(8,128)S(1)} %add_select_fusion.3), channel_id=1, source_target_pairs={{0,64},{8,72},{16,80},{24,88},{32,96},{40,104},{48,112},{56,120},{... | collective-permute-start | bytes 3145736 | tf_op jit(solution)/shard_map/ppermute | solution.py:11
  142.0 39.4 %copy-start = (s32[1024]{0:T(1024)S(1)}, s32[1024]{0:T(1024)}, u32[]{:S(2)}) copy-start(s32[1024]{0:T(1024)} %param.6) | copy-start | bytes 12292
  142.1 24.4 %collective-permute-start.4 = (f32[128,2048]{1,0:T(8,128)S(1)}, f32[128,2048]{1,0:T(8,128)S(1)}, u32[]{:S(2)}, u32[]{:S(2)}) collective-permute-start(f32[128,2048]{1,0:T(8,128)S(1)} %add_select_fusion.2), channel_id=1, source_target_pairs={{0,128},{8,136},{16,144},{24,152},{32,160},{40,168},{48,176},{56,1... | collective-permute-start | bytes 3145736 | tf_op jit(solution)/shard_map/ppermute | solution.py:11
  166.6 35.3 %collective-permute-start.5 = (f32[128,2048]{1,0:T(8,128)S(1)}, f32[128,2048]{1,0:T(8,128)S(1)}, u32[]{:S(2)}, u32[]{:S(2)}) collective-permute-start(f32[128,2048]{1,0:T(8,128)S(1)} %add_select_fusion.1), channel_id=1, source_target_pairs={{0,256},{8,264},{16,272},{24,280},{32,288},{40,296},{48,304},{56,3... | collective-permute-start | bytes 3145736 | tf_op jit(solution)/shard_map/ppermute | solution.py:11
  205.2 1.1 copy-start.1
  206.3 1196.8 %reduce-scatter.2.cloned.1.call-start = ((), (), s32[]{:S(2)}) async-start(), calls=%async_computation.2 | async-start | bytes 2359296 | tf_op jit(solution)/shard_map/reduce_scatter | solution.py:58
Sparse Core Ops, SparseCore 0:
  206.5 1084.4 all-reduce.1
  1294.1 108.9 reduce-scatter.1
where the time goes:
time: 1410 us
  waiting for transfers between devices  1320 us (94%)
  starting transfers between devices  42.2 us (3%)
  matrix products  25.3 us (2%)
    psum x1, waiting for transfers between devices, body(): combined = lax.psum(jnp.where(owned, picked, 0.0), 'feat')  1080 us
    ppermute x6, waiting for transfers between devices, from_partner(): lax.ppermute(array, axis, [(i, i ^ 1 << distance) for i in range(lax.axis...  128 us
    reduce_scatter x1, waiting for transfers between devices, body(): lax.psum_scatter(partial_gram.reshape(C // tok_count * lax.axis_size('tok...  109 us
    ppermute x6, starting transfers between devices, from_partner(): lax.ppermute(array, axis, [(i, i ^ 1 << distance) for i in range(lax.axis...  42.1 us
  transfers between devices with their start and end apart: 8, of which 8 were waited for; matrix products, arithmetic and copies ran while one was open for 0% of the time, Pallas kernels for 0%

commit v1 on v0

--- a/solution.py
+++ b/solution.py
@@ -45,7 +45,7 @@
         transformed = jnp.where(upper, partner - transformed, transformed + partner)
     picked = jnp.take(transformed, local_col, axis=1)
     owned = (owner == feat_index)[None, :]
-    combined = lax.psum(jnp.where(owned, picked, 0.0), "feat")
+    combined = jnp.sum(lax.all_gather(jnp.where(owned, picked, 0.0), "feat"), axis=0)
     sketch = (combined * (1.0 / math.sqrt(width * feat_count))).astype(jnp.bfloat16)
     factor = C / (rows * tok_count)
     own_rows = lax.dynamic_slice_in_dim(sketch, feat_index * shard_cols, shard_cols, 1)

time: 1410 us -> 767 us (0.54)
  the two profiles are of different devices: /device:TPU:12 before, /device:TPU:4 now
where the time goes in v1:
time: 767 us
  waiting for transfers between devices  655 us (85%)
  starting transfers between devices  54.9 us (7%)
  matrix products  25.3 us (3%)
  other arithmetic  13.8 us (2%)
  between operations  13.6 us (2%)
    all_gather x1, waiting for transfers between devices, body(): lax.all_gather(jnp.where(owned, picked, 0.0), 'feat')  438 us
    ppermute x6, waiting for transfers between devices, from_partner(): lax.ppermute(array, axis, [(i, i ^ 1 << distance) for i in range(lax.axis...  126 us
    reduce_scatter x1, waiting for transfers between devices, body(): lax.psum_scatter(partial_gram.reshape(C // tok_count * lax.axis_size('tok...  89.7 us
    ppermute x6, starting transfers between devices, from_partner(): lax.ppermute(array, axis, [(i, i ^ 1 << distance) for i in range(lax.axis...  54.8 us
    dot_general x1, matrix products, body(): jnp.dot(signed, sylvester(width, jnp.bfloat16), preferred_element_type=jn...  23.5 us
  transfers between devices with their start and end apart: 8, of which 8 were waited for; matrix products, arithmetic and copies ran while one was open for 0% of the time, Pallas kernels for 0%

profile of v1, /device:TPU:4, one launch (start us, length us, event | category | flops | bytes accessed | tf_op | source)
XLA Modules:
  0.0 766.6 jit_solution(306146808236919150)
XLA Ops:
  6.5 0.7 convert_element_type.17
  7.2 23.5 %fusion = f32[128,2048]{1,0:T(8,128)S(1)} fusion(bf16[128,2048]{1,0:T(8,128)(2,1)} %param.4, bf16[2048]{0:T(1024)(128)(2,1)S(1)} %convert_element_type.17), kind=kOutput, calls=%fused_computation.2 | convolution fusion | flops 1237581824 | bytes 1576960 | tf_op jit(solution)/shard_map/dot_general | solution.py:36
  30.8 1.9 collective-permute-start
  32.7 2.6 collective-permute-done
  35.5 3.5 collective-permute-start.1
  39.0 23.6 %collective-permute-done.1 = f32[128,2048]{1,0:T(8,128)S(1)} collective-permute-done((f32[128,2048]{1,0:T(8,128)S(1)}, f32[128,2048]{1,0:T(8,128)S(1)}, u32[]{:S(2)}, u32[]{:S(2)}) %collective-permute-start.1) | collective-permute-done | bytes 1048608 | tf_op jit(solution)/shard_map/ppermute | solution.py:11
  62.6 0.1 add_select_fusion.4
  62.7 5.3 collective-permute-start.2
  68.1 22.4 %collective-permute-done.2 = f32[128,2048]{1,0:T(8,128)S(1)} collective-permute-done((f32[128,2048]{1,0:T(8,128)S(1)}, f32[128,2048]{1,0:T(8,128)S(1)}, u32[]{:S(2)}, u32[]{:S(2)}) %collective-permute-start.2) | collective-permute-done | bytes 1048608 | tf_op jit(solution)/shard_map/ppermute | solution.py:11
  90.7 15.7 %collective-permute-start.3 = (f32[128,2048]{1,0:T(8,128)S(1)}, f32[128,2048]{1,0:T(8,128)S(1)}, u32[]{:S(2)}, u32[]{:S(2)}) collective-permute-start(f32[128,2048]{1,0:T(8,128)S(1)} %add_select_fusion.3), channel_id=1, source_target_pairs={{0,64},{8,72},{16,80},{24,88},{32,96},{40,104},{48,112},{56,120},{... | collective-permute-start | bytes 3145736 | tf_op jit(solution)/shard_map/ppermute | solution.py:11
  106.4 35.5 %collective-permute-done.3 = f32[128,2048]{1,0:T(8,128)S(1)} collective-permute-done((f32[128,2048]{1,0:T(8,128)S(1)}, f32[128,2048]{1,0:T(8,128)S(1)}, u32[]{:S(2)}, u32[]{:S(2)}) %collective-permute-start.3) | collective-permute-done | bytes 1048608 | tf_op jit(solution)/shard_map/ppermute | solution.py:11
  142.1 3.1 collective-permute-start.4
  145.2 21.3 %collective-permute-done.4 = f32[128,2048]{1,0:T(8,128)S(1)} collective-permute-done((f32[128,2048]{1,0:T(8,128)S(1)}, f32[128,2048]{1,0:T(8,128)S(1)}, u32[]{:S(2)}, u32[]{:S(2)}) %collective-permute-start.4) | collective-permute-done | bytes 1048608 | tf_op jit(solution)/shard_map/ppermute | solution.py:11
  166.6 25.2 %collective-permute-start.5 = (f32[128,2048]{1,0:T(8,128)S(1)}, f32[128,2048]{1,0:T(8,128)S(1)}, u32[]{:S(2)}, u32[]{:S(2)}) collective-permute-start(f32[128,2048]{1,0:T(8,128)S(1)} %add_select_fusion.1), channel_id=1, source_target_pairs={{0,256},{8,264},{16,272},{24,280},{32,288},{40,296},{48,304},{56,3... | collective-permute-start | bytes 3145736 | tf_op jit(solution)/shard_map/ppermute | solution.py:11
  191.9 21.0 %collective-permute-done.5 = f32[128,2048]{1,0:T(8,128)S(1)} collective-permute-done((f32[128,2048]{1,0:T(8,128)S(1)}, f32[128,2048]{1,0:T(8,128)S(1)}, u32[]{:S(2)}, u32[]{:S(2)}) %collective-permute-start.5) | collective-permute-done | bytes 1048608 | tf_op jit(solution)/shard_map/ppermute | solution.py:11
  213.1 0.3 copy.7
  213.4 2.8 gather_fusion
  216.2 0.3 fusion.1
  216.6 1.0 copy.8
  217.7 438.5 %all-gather.2.cloned.1.call-done = f32[64,128,1024]{2,1,0:T(8,128)} async-done(((f32[1,128,1024]{2,1,0:T(8,128)}), f32[64,128,1024]{2,1,0:T(8,128)}) %all-gather.2.cloned.1.call-update) | async-done | bytes 33554448 | tf_op jit(solution)/shard_map/all_gather | solution.py:48
  656.2 11.8 %reduce_sum.9 = f32[128,1024]{1,0:T(8,128)S(1)} reduce(f32[64,128,1024]{2,1,0:T(8,128)} %all-gather.2.cloned.1.call-done, f32[]{:T(128)} %constant.79.clone.1), dimensions={0}, to_apply=%region_0.1 | reduce | flops 8257536 | bytes 34078724 | tf_op jit(solution)/shard_map/reduce_sum | solution.py:48
  668.0 0.2 copy.13
  668.2 1.8 convolution_multiply_fusion
  670.0 89.7 %reduce-scatter.2.cloned.1.call-done = f32[4,16,1024]{2,1,0:T(8,128)} async-done(((f32[32,16,1024]{2,1,0:T(8,128)}), f32[4,16,1024]{2,1,0:T(8,128)}) %reduce-scatter.2.cloned.1.call-update) | async-done | bytes 262160 | tf_op jit(solution)/shard_map/reduce_scatter | solution.py:58
  (18 shorter events, 0.9 us)
Async XLA Ops:
  6.5 649.6 %all-gather.2.cloned.1.call-start = ((), (), s32[]{:S(2)}) async-start(), calls=%async_computation.1 | async-start | bytes 34078720 | tf_op jit(solution)/shard_map/all_gather | solution.py:48
  7.2 184.7 %copy-start = (s32[1024]{0:T(1024)S(1)}, s32[1024]{0:T(1024)}, u32[]{:S(2)}) copy-start(s32[1024]{0:T(1024)} %param.6) | copy-start | bytes 12292
  30.8 186.9 %copy-start.1 = (s32[128,1]{0,1:T(1,128)S(1)}, s32[128,1]{0,1:T(1,128)}, u32[]{:S(2)}) copy-start(s32[128,1]{0,1:T(1,128)} %param.7) | copy-start | bytes 1540
  30.8 4.6 collective-permute-start
  35.5 27.1 %collective-permute-start.1 = (f32[128,2048]{1,0:T(8,128)S(1)}, f32[128,2048]{1,0:T(8,128)S(1)}, u32[]{:S(2)}, u32[]{:S(2)}) collective-permute-start(f32[128,2048]{1,0:T(8,128)S(1)} %add_select_fusion.5), channel_id=1, source_target_pairs={{0,16},{8,24},{16,0},{24,8},{32,48},{40,56},{48,32},{56,40},{64,80... | collective-permute-start | bytes 3145736 | tf_op jit(solution)/shard_map/ppermute | solution.py:11
  62.7 27.8 %collective-permute-start.2 = (f32[128,2048]{1,0:T(8,128)S(1)}, f32[128,2048]{1,0:T(8,128)S(1)}, u32[]{:S(2)}, u32[]{:S(2)}) collective-permute-start(f32[128,2048]{1,0:T(8,128)S(1)} %add_select_fusion.4), channel_id=1, source_target_pairs={{0,32},{8,40},{16,48},{24,56},{32,0},{40,8},{48,16},{56,24},{64,96... | collective-permute-start | bytes 3145736 | tf_op jit(solution)/shard_map/ppermute | solution.py:11
  90.7 51.2 %collective-permute-start.3 = (f32[128,2048]{1,0:T(8,128)S(1)}, f32[128,2048]{1,0:T(8,128)S(1)}, u32[]{:S(2)}, u32[]{:S(2)}) collective-permute-start(f32[128,2048]{1,0:T(8,128)S(1)} %add_select_fusion.3), channel_id=1, source_target_pairs={{0,64},{8,72},{16,80},{24,88},{32,96},{40,104},{48,112},{56,120},{... | collective-permute-start | bytes 3145736 | tf_op jit(solution)/shard_map/ppermute | solution.py:11
  142.1 24.4 %collective-permute-start.4 = (f32[128,2048]{1,0:T(8,128)S(1)}, f32[128,2048]{1,0:T(8,128)S(1)}, u32[]{:S(2)}, u32[]{:S(2)}) collective-permute-start(f32[128,2048]{1,0:T(8,128)S(1)} %add_select_fusion.2), channel_id=1, source_target_pairs={{0,128},{8,136},{16,144},{24,152},{32,160},{40,168},{48,176},{56,1... | collective-permute-start | bytes 3145736 | tf_op jit(solution)/shard_map/ppermute | solution.py:11
  166.6 46.3 %collective-permute-start.5 = (f32[128,2048]{1,0:T(8,128)S(1)}, f32[128,2048]{1,0:T(8,128)S(1)}, u32[]{:S(2)}, u32[]{:S(2)}) collective-permute-start(f32[128,2048]{1,0:T(8,128)S(1)} %add_select_fusion.1), channel_id=1, source_target_pairs={{0,256},{8,264},{16,272},{24,280},{32,288},{40,296},{48,304},{56,3... | collective-permute-start | bytes 3145736 | tf_op jit(solution)/shard_map/ppermute | solution.py:11
  217.6 542.1 %reduce-scatter.2.cloned.1.call-start = ((), (), s32[]{:S(2)}) async-start(), calls=%async_computation.2 | async-start | bytes 2359296 | tf_op jit(solution)/shard_map/reduce_scatter | solution.py:58
Sparse Core Ops, SparseCore 0:
  217.7 438.3 all-gather.1
  670.2 89.5 reduce-scatter.1
